TPU v7x, 512 devices: a whole 4x8x8 slice. The times are simulated.
512 devices in a mesh: dp: 8 (over y_hi, core), mp: 64 (over z, x, y_lo).
Axes of the slice: x: 4, y: 8 (y_hi: 4, y_lo: 2; y = y_hi * 2 + y_lo), z: 8, core: 2. Of those that a mesh axis runs over, the one named last changes fastest.
Arguments:
- queries: bfloat16 [65536, 768], P(('dp', 'mp')), may hold values from -30 to 30
- first_owner: int32 [65536, 1], P(('dp', 'mp')), may hold values from 0 to 63; in each aligned block of 128 rows (0 to 127, 128 to 255, ...) at most 4 rows name the same one
- first_row: int32 [65536], P(('dp', 'mp')), may hold values from 0 to 255
- tool_table: bfloat16 [16384, 768], P('mp'), may hold values from -6 to 6
- norm_gain: bfloat16 [768], replicated, may hold values from 0.25 to 1.75
- weight_in: bfloat16 [3072, 768], P('mp'), may hold values from -0.21875 to 0.21875
- bias_in: bfloat16 [3072], P('mp'), may hold values from -3 to 3
- weight_out: bfloat16 [3072, 768], P('mp'), may hold values from -0.109375 to 0.109375
- bias_out: bfloat16 [768], replicated, may hold values from -3 to 3
- tool_embeds: bfloat16 [512, 768], P('dp'), may hold values from -2 to 2
- positive: int32 [65536], P(('dp', 'mp')), may hold values from 0 to 511
Outputs:
- updated: bfloat16 [65536, 768], P(('dp', 'mp'))
- chain_loss: float32 [65536], P(('dp', 'mp'))
- query_grad: float32 [65536, 768], P(('dp', 'mp'))
- tool_grad: float32 [512, 768], P('dp')
Inputs may be any that keep to these rules, and one draw needn't show every extreme that they name: `first_owner`: among the 128 chains of one device at most 4 name the same owner, a bound that some block reaches of them.
All inputs are finite; a program needn't handle non-finite values.
Results may differ from a plain program's by a relative error of at most 0.0078.
Values may be sent and summed in bfloat16 or wider, within the bound.
A program may use at most 64 MiB of HBM per device.

v0:
```python
import jax
import jax.numpy as jnp
import numpy as np
from jax import lax
from jax.sharding import PartitionSpec as P


def from_behind(block, axis, distance):
    devices = range(lax.axis_size(axis))
    route = [((i - distance) % len(devices), i) for i in devices]
    return lax.ppermute(block, axis, route)


def layer_normed(combined, norm_gain):
    row_mean = jnp.mean(combined, axis=1, keepdims=True)
    centred = combined - row_mean
    spread = jnp.mean(centred * centred, axis=1, keepdims=True)
    return (centred * lax.rsqrt(spread + 1e-05) * norm_gain.astype(jnp.float32)[None, :]).astype(
        jnp.bfloat16
    )


def hidden_terms(pieces, normed):
    in_piece, bias_piece, out_piece = pieces
    preact = lax.dot_general(
        normed, in_piece, (((1,), (1,)), ((), ())), preferred_element_type=jnp.float32
    )
    preact = preact + bias_piece.astype(jnp.float32)[None, :]
    activated = jax.nn.gelu(preact, approximate=True).astype(jnp.bfloat16)
    return jnp.dot(activated, out_piece, preferred_element_type=jnp.float32)


def local(
    queries,
    first_owner,
    first_row,
    tool_table,
    norm_gain,
    weight_in,
    bias_in,
    weight_out,
    bias_out,
    tool_embeds,
    positive,
):
    chain_count, feature_count = queries.shape
    groups = lax.axis_size("mp")
    cycle_size = lax.axis_size("dp")
    cycle_index = lax.axis_index("dp")
    capacity = 2 * chain_count // groups
    owner_ids = first_owner[:, 0]
    owner_marks = (owner_ids[:, None] == jnp.arange(groups, dtype=jnp.int32)[None, :]).astype(
        jnp.int32
    )
    rank_in_owner = jnp.sum((jnp.cumsum(owner_marks, axis=0) - owner_marks) * owner_marks, axis=1)
    slot_index = owner_ids * capacity + rank_in_owner
    request = (
        jnp.zeros((groups * capacity,), jnp.int32)
        .at[slot_index]
        .set(first_row)
        .reshape(groups, capacity)
    )
    table_rows = jnp.take(
        tool_table, lax.all_to_all(request, "mp", split_axis=0, concat_axis=0, tiled=True), axis=0
    )
    fetched = lax.all_to_all(table_rows, "mp", split_axis=0, concat_axis=0, tiled=True)
    first_rows = fetched.reshape(groups * capacity, feature_count)[slot_index]
    combined = queries.astype(jnp.float32) + first_rows.astype(jnp.float32)
    normed = layer_normed(combined, norm_gain)
    branch_sum = hidden_terms(
        (
            lax.all_gather(weight_in, "mp", axis=0, tiled=True),
            lax.all_gather(bias_in, "mp", axis=0, tiled=True),
            lax.all_gather(weight_out, "mp", axis=0, tiled=True),
        ),
        normed,
    )
    updated = (combined + branch_sum + bias_out.astype(jnp.float32)[None, :]).astype(jnp.bfloat16)
    block_rows = tool_embeds.shape[0]
    forward_hops = cycle_size - 1
    block_list = [tool_embeds]
    offset_list = [0]
    visiting = tool_embeds
    for hop_number in range(forward_hops):
        visiting = from_behind(visiting, "dp", 1)
        block_list.append(visiting)
        offset_list.append(hop_number + 1)
    all_tools = jnp.concatenate(block_list, axis=0)
    block_owner = (cycle_index - jnp.asarray(offset_list, jnp.int32)) % cycle_size
    column_ids = (
        block_owner[:, None] * block_rows + jnp.arange(block_rows, dtype=jnp.int32)[None, :]
    ).reshape(-1)
    scores = lax.dot_general(
        updated, all_tools, (((1,), (1,)), ((), ())), preferred_element_type=jnp.float32
    )
    row_max = jnp.max(scores, axis=1, keepdims=True)
    log_total = row_max + jnp.log(jnp.sum(jnp.exp(scores - row_max), axis=1, keepdims=True))
    is_positive = (column_ids[None, :] == positive[:, None]).astype(jnp.float32)
    chain_loss = log_total[:, 0] - jnp.sum(scores * is_positive, axis=1)
    weights_grad = (jnp.exp(scores - log_total) - is_positive).astype(jnp.bfloat16)
    query_grad = jnp.dot(weights_grad, all_tools, preferred_element_type=jnp.float32)
    position_of = np.zeros((cycle_size,), np.int32)
    for list_index, offset_value in enumerate(offset_list):
        position_of[offset_value] = list_index

    def block_term(offset_value):
        list_index = int(position_of[offset_value])
        columns = weights_grad[:, list_index * block_rows : (list_index + 1) * block_rows]
        return lax.dot_general(
            columns, updated, (((0,), (0,)), ((), ())), preferred_element_type=jnp.float32
        )

    partial_grad = jnp.zeros((block_rows, feature_count), jnp.float32)
    for hop_number in range(cycle_size - 1):
        partial_grad = partial_grad + block_term(hop_number + 1)
        partial_grad = from_behind(partial_grad.astype(jnp.bfloat16), "dp", 1).astype(
            partial_grad.dtype
        )
    partial_grad = partial_grad + block_term(0)
    grad_scale = (block_rows * cycle_size / (chain_count * groups * cycle_size)) ** 0.5
    tool_grad = lax.psum(partial_grad, "mp") * grad_scale
    return (updated, chain_loss, query_grad, tool_grad)


def solution(mesh):
    in_specs = (
        P(("dp", "mp"), None),
        P(("dp", "mp"), None),
        P(("dp", "mp")),
        P("mp", None),
        P(),
        P("mp", None),
        P("mp"),
        P("mp", None),
        P(),
        P("dp", None),
        P(("dp", "mp")),
    )
    out_specs = (P(("dp", "mp"), None), P(("dp", "mp")), P(("dp", "mp"), None), P("dp", None))
    return jax.shard_map(local, mesh=mesh, in_specs=in_specs, out_specs=out_specs, check_vma=False)
```

profile of v0, /device:TPU:2, one launch (start us, length us, event | category | flops | bytes accessed | tf_op | source)
XLA Modules:
  0.0 1265.2 jit_solution(13888815105655201328)
XLA Ops:
  12.9 14.9 %all-to-all-start = ((s32[64,1,4]{2,1,0:T(1,128)}), s32[64,1,4]{2,1,0:T(1,128)S(1)}, u32[]{:S(2)}, u32[]{:S(2)}) async-start(s32[64,1,4]{2,1,0:T(1,128)} %bitcast.3), calls=%async_computation | async-start | bytes 65536 | tf_op jit(solution)/shard_map/all_to_all | solution.py:64
  27.8 1.9 collective-permute-start
  33.5 159.0 %all-reduce = bf16[3072]{0:T(1024)(128)(2,1)S(1)} all-reduce(bf16[3072]{0:T(1024)(128)(2,1)S(1)} %dynamic-update-slice), channel_id=1, replica_groups=mesh['dp'=8,'mp'=64] {'mp'}, use_global_device_ids=true, to_apply=%add | all-reduce | flops 3072 | bytes 12288
  196.4 9.7 all-to-all-start.1
  206.2 1.9 collective-permute-start.1
  208.2 8.4 collective-permute-done.1
  216.6 1.9 collective-permute-start.2
  218.5 8.0 collective-permute-done.2
  226.5 1.9 collective-permute-start.3
  228.4 7.3 collective-permute-done.3
  235.7 1.9 collective-permute-start.4
  237.7 7.8 collective-permute-done.4
  247.4 6.5 collective-permute-done.5
  255.8 7.1 collective-permute-done.6
  264.3 68.5 %all-gather.3.cloned.1.call-done = bf16[3072,768]{1,0:T(8,128)(2,1)} async-done(((bf16[48,768]{1,0:T(8,128)(2,1)}), bf16[3072,768]{1,0:T(8,128)(2,1)}) %all-gather.3.cloned.1.call-update) | async-done | bytes 4718608 | tf_op jit(solution)/shard_map/all_gather | solution.py:72
  332.8 312.7 %all-gather.5.cloned.1.call-done = bf16[3072,768]{1,0:T(8,128)(2,1)} async-done(((bf16[48,768]{1,0:T(8,128)(2,1)}), bf16[3072,768]{1,0:T(8,128)(2,1)}) %all-gather.5.cloned.1.call-update) | async-done | bytes 4718608 | tf_op jit(solution)/shard_map/all_gather | solution.py:74
  645.6 6.2 fusion.9
  653.4 1.9 collective-permute-start.7
  655.3 6.1 collective-permute-done.7
  661.7 1.9 collective-permute-start.8
  663.8 5.9 collective-permute-done.8
  669.7 1.9 collective-permute-start.9
  671.8 5.9 collective-permute-done.9
  677.8 1.9 collective-permute-start.10
  680.0 5.9 collective-permute-done.10
  685.9 1.9 collective-permute-start.11
  688.0 7.0 collective-permute-done.11
  695.0 1.9 collective-permute-start.12
  697.2 6.7 collective-permute-done.12
  703.9 1.9 collective-permute-start.13
  706.0 5.9 collective-permute-done.13
  713.7 543.3 %all-reduce.3.cloned.1.call-done = f32[64,768]{1,0:T(8,128)} async-done(((f32[64,768]{1,0:T(8,128)}), f32[64,768]{1,0:T(8,128)}) %all-reduce.3.cloned.1.call-update) | async-done | bytes 196624 | tf_op jit(solution)/shard_map/psum | solution.py:121
  (76 shorter events, 24.5 us)
Async XLA Ops:
  7.2 186.9 %copy-start = (bf16[256,768]{1,0:T(8,128)(2,1)S(1)}, bf16[256,768]{1,0:T(8,128)(2,1)}, u32[]{:S(2)}) copy-start(bf16[256,768]{1,0:T(8,128)(2,1)} %param.15) | copy-start | bytes 1179652
  7.2 325.6 %all-gather.3.cloned.1.call-start = ((), (), s32[]{:S(2)}) async-start(), calls=%async_computation.2 | async-start | bytes 4792320 | tf_op jit(solution)/shard_map/all_gather | solution.py:72
  7.9 637.6 %all-gather.5.cloned.1.call-start = ((), (), s32[]{:S(2)}) async-start(), calls=%async_computation.3 | async-start | bytes 4792320 | tf_op jit(solution)/shard_map/all_gather | solution.py:74
  12.9 181.0 %all-to-all-start = ((s32[64,1,4]{2,1,0:T(1,128)}), s32[64,1,4]{2,1,0:T(1,128)S(1)}, u32[]{:S(2)}, u32[]{:S(2)}) async-start(s32[64,1,4]{2,1,0:T(1,128)} %bitcast.3), calls=%async_computation | async-start | bytes 65536 | tf_op jit(solution)/shard_map/all_to_all | solution.py:64
  27.8 178.4 %collective-permute-start = (bf16[64,768]{1,0:T(8,128)(2,1)}, bf16[64,768]{1,0:T(8,128)(2,1)S(1)}, u32[]{:S(2)}, u32[]{:S(2)}) collective-permute-start(bf16[64,768]{1,0:T(8,128)(2,1)} %param.21), channel_id=1, source_target_pairs={{448,0},{0,64},{64,128},{128,192},{192,256},{256,320},{320,384},{3... | collective-permute-start | bytes 294920 | tf_op jit(solution)/shard_map/ppermute | solution.py:11
  196.4 66.5 %all-to-all-start.1 = ((bf16[64,4,768]{2,1,0:T(4,128)(2,1)}), bf16[64,4,768]{2,1,0:T(4,128)(2,1)S(1)}, u32[]{:S(2)}, u32[]{:S(2)}) async-start(bf16[64,4,768]{2,1,0:T(4,128)(2,1)} %broadcast_select_fusion), calls=%async_computation.1 | async-start | bytes 786432 | tf_op jit(solution)/shard_map/all_to_all | solution.py:66
  206.1 1050.9 %all-reduce.3.cloned.1.call-start = ((), (), s32[]{:S(2)}) async-start(), calls=%async_computation.4 | async-start | bytes 393216 | tf_op jit(solution)/shard_map/psum | solution.py:121
  206.2 10.4 collective-permute-start.1
  216.6 9.9 collective-permute-start.2
  226.5 9.2 collective-permute-start.3
  235.7 9.7 collective-permute-start.4
  237.6 26.3 %copy-start.2 = (bf16[128,768]{1,0:T(8,128)(2,1)S(1)}, bf16[128,768]{1,0:T(8,128)(2,1)}, u32[]{:S(2)}) copy-start(bf16[128,768]{1,0:T(8,128)(2,1)} %param.12) | copy-start | bytes 589828
  245.4 8.4 collective-permute-start.5
  253.9 9.1 collective-permute-start.6
  264.3 388.0 %copy-start.3 = (s32[128]{0:T(128)S(1)}, s32[128]{0:T(128)}, u32[]{:S(2)}) copy-start(s32[128]{0:T(128)} %param.22) | copy-start | bytes 1540
  651.8 54.1 %copy-start.1 = (bf16[128,768]{1,0:T(8,128)(2,1)}, bf16[128,768]{1,0:T(8,128)(2,1)S(1)}, u32[]{:S(2)}) copy-start(bf16[128,768]{1,0:T(8,128)(2,1)S(1)} %fusion.9) | copy-start | bytes 589828
  653.4 8.0 collective-permute-start.7
  661.7 8.0 collective-permute-start.8
  669.7 8.0 collective-permute-start.9
  677.8 8.0 collective-permute-start.10
  685.9 9.1 collective-permute-start.11
  695.0 8.9 collective-permute-start.12
  703.9 8.0 collective-permute-start.13
Sparse Core Ops, SparseCore 0:
  10.1 322.6 all-gather.2
  334.9 310.6 all-gather.4
  712.8 544.1 all-reduce.2
where the time goes:
time: 1270 us
  waiting for transfers between devices  1010 us (80%)
  blocking collectives  159 us (13%)
  starting transfers between devices  51.5 us (4%)
  between operations  14.8 us (1%)
    psum x1, waiting for transfers between devices, local(): tool_grad = lax.psum(partial_grad, 'mp') * grad_scale  543 us
    all_gather x1, waiting for transfers between devices, local(): lax.all_gather(weight_out, 'mp', axis=0, tiled=True)  313 us
    unnamed x1, blocking collectives  159 us
    ppermute x14, waiting for transfers between devices, from_behind(): return lax.ppermute(block, axis, route)  88.5 us
    all_gather x1, waiting for transfers between devices, local(): lax.all_gather(weight_in, 'mp', axis=0, tiled=True)  68.5 us
    ppermute x14, starting transfers between devices, from_behind(): return lax.ppermute(block, axis, route)  26.8 us
  transfers between devices with their start and end apart: 19, of which 16 were waited for; matrix products, arithmetic and copies ran while one was open for 1% of the time, Pallas kernels for 0%

commit v1 on v0

v1 whole, which is shorter than its diff:
```python
import functools

import jax
import jax.numpy as jnp
from jax import lax
from jax.experimental import pallas as pl
from jax.experimental.pallas import tpu as pltpu
from jax.sharding import PartitionSpec as P

MESH = pl.DeviceIdType.MESH
BF, F32, I32 = jnp.bfloat16, jnp.float32, jnp.int32
NZ, NX, NYL, NYH, NC = 8, 4, 2, 4, 2
NP = NX * NYL
CAP = 4
N_SEMS = 192


def iota(shape, axis):
    return lax.broadcasted_iota(I32, shape, axis)


def bits(mask):
    return jnp.where(mask, 1.0, 0.0).astype(BF)


def dot(a, b):
    return jnp.dot(a, b, preferred_element_type=F32)


def dot_t(a, b):
    return lax.dot_general(a, b, (((1,), (1,)), ((), ())), preferred_element_type=F32)


def gelu(u):
    return 0.5 * u * (1.0 + jnp.tanh(0.7978845608028654 * (u + 0.044715 * (u * u * u))))


def kernel(
    grad_scale,
    queries,
    owner_ref,
    row_ref,
    table,
    gain,
    w_in,
    bias_in,
    w_out,
    bias_out,
    tools,
    positive,
    updated_ref,
    loss_ref,
    qgrad_ref,
    tgrad_ref,
    winb,
    woutb,
    toolsb,
    req1,
    rcv1,
    req2,
    rcv2,
    g1b,
    ra,
    bb,
    fb,
    nbuf,
    pbuf,
    rbuf,
    updb,
    wgb,
    wga,
    s1b,
    s1r,
    s2b,
    s2r,
    s3b,
    s3r,
    s4r,
    send_sems,
    recv_sems,
    local_sems,
):
    d, m = lax.axis_index("dp"), lax.axis_index("mp")
    yh, c = lax.div(d, NC), lax.rem(d, NC)
    z, p = lax.div(m, NP), lax.rem(m, NP)
    x, yl = lax.div(p, NYL), lax.rem(p, NYL)
    chains = queries.shape[0]

    def z_peer(o):
        return {"mp": lax.rem(z + o, NZ) * NP + p}

    def p_peer(o):
        return {"mp": z * NP + lax.rem(p + o, NP)}

    def x_peer(o):
        return {"mp": z * NP + lax.rem(x + o, NX) * NYL + yl}

    def y_peer(o):
        return {"dp": lax.rem(yh + o, NYH) * NC + c}

    other_core = {"dp": yh * NC + (1 - c)}
    y_flip = {"mp": z * NP + x * NYL + (1 - yl)}
    z_next = {"mp": lax.rem(z + 1 + (NZ - 2) * c, NZ) * NP + p}
    z_prev = {"mp": lax.rem(z + (NZ - 1) - (NZ - 2) * c, NZ) * NP + p}
    x_next = {"mp": z * NP + lax.rem(x + 1 + (NX - 2) * c, NX) * NYL + yl}
    x_prev = {"mp": z * NP + lax.rem(x + (NX - 1) - (NX - 2) * c, NX) * NYL + yl}

    def zb(k):
        return lax.rem(z - k + 2 * k * c + NZ, NZ)

    def xb(k):
        return lax.rem(x - k + 2 * k * c + NX, NX)

    count = [0]
    started = []

    def remote(src, dst, peer):
        i = count[0]
        count[0] += 1
        return pltpu.make_async_remote_copy(
            src_ref=src,
            dst_ref=dst,
            send_sem=send_sems.at[i],
            recv_sem=recv_sems.at[i],
            device_id=peer,
            device_id_type=MESH,
        )

    def send(src, dst, peer):
        copy = remote(src, dst, peer)
        copy.start()
        started.append(copy)
        return copy

    def arrive(copies):
        for copy in copies:
            copy.wait_recv()

    barrier = pltpu.get_barrier_semaphore()
    peers = [z_peer(o) for o in range(1, NZ)] + [p_peer(o) for o in range(1, NP)]
    peers += [y_peer(o) for o in range(1, NYH)] + [other_core]
    for peer in peers:
        pl.semaphore_signal(barrier, inc=1, device_id=peer, device_id_type=MESH)
    pl.semaphore_wait(barrier, len(peers))

    y_in = remote(w_in, winb.at[z, x], y_flip)
    y_out = remote(w_out, woutb.at[z, x], y_flip)
    own_in = pltpu.make_async_copy(w_in, winb.at[z, x], local_sems.at[0])
    own_out = pltpu.make_async_copy(w_out, woutb.at[z, x], local_sems.at[1])

    @pl.when(c == yl)
    def _():
        y_in.start()
        y_out.start()
        own_in.start()
        own_out.start()

    own_tools = pltpu.make_async_copy(tools, toolsb.at[c * NYH + yh], local_sems.at[2])
    own_tools.start()
    tool_sends = [send(tools, toolsb.at[c * NYH + yh], y_peer(o)) for o in range(1, NYH)]
    tool_swaps = [send(tools, toolsb.at[c * NYH + yh], other_core)]

    owner = owner_ref[...]
    eye = iota((chains, chains), 0) == iota((chains, chains), 1)
    own_mask = owner == iota((chains, NZ * NP), 1)
    earlier = bits(iota((chains, chains), 1) < iota((chains, chains), 0))
    prior = dot(earlier, bits(own_mask))
    rank = jnp.sum(jnp.where(own_mask, prior, 0.0), axis=1, keepdims=True).astype(I32)
    row_col = jnp.sum(jnp.where(eye, row_ref[...].astype(F32), 0.0), axis=1, keepdims=True)
    owner_row = jnp.sum(jnp.where(eye, owner.astype(F32), 0.0), axis=0, keepdims=True).astype(I32)
    lane_of = (owner & (NP - 1)) * CAP + rank
    spread = jnp.where(iota((chains, 128), 1) == lane_of, row_col, 0.0).astype(BF)
    to_z = bits((owner_row >> 3) == iota((16, chains), 0))
    bias_line = jnp.where(iota((16, 128), 0) == NZ, bias_in[...].astype(F32), 0.0)
    req1[...] = dot(to_z, spread) + bias_line
    rcv1[z] = req1[...]
    reqs1 = [send(req1, rcv1.at[z], z_peer(o)) for o in range(1, NZ)]

    @pl.when(c == yl)
    def _():
        own_in.wait()
        own_out.wait()

    @pl.when(c != yl)
    def _():
        y_in.wait_recv()
        y_out.wait_recv()

    a_x = {NX - o: send(winb.at[z, x], winb.at[z, x], x_peer(o)) for o in range(1, NX)}
    a_next, a_prev, b_next, b_prev, b_x = {}, {}, {}, {}, {}

    def a_step(k, j):
        xj = lax.rem(x + j, NX)
        if k == 1 and j > 0:
            a_x[j].wait_recv()
        if k > 1:
            a_next[k - 1, j].wait_recv()
        src = winb.at[zb(k - 1), xj]
        a_next[k, j] = send(src, src, z_next)
        if k <= 3:
            if k > 1:
                a_prev[k - 1, j].wait_recv()
            src = winb.at[zb(1 - k), xj]
            a_prev[k, j] = send(src, src, z_prev)

    def b_cross(k):
        src = woutb.at[zb(k), x]
        b_x[k, 1] = send(src, src, x_next)
        b_x[k, -1] = send(src, src, x_prev)

    def b_relay(k):
        b_x[k, 1].wait_recv()
        src = woutb.at[zb(k), xb(1)]
        b_x[k, 2] = send(src, src, x_next)

    def b_step(k):
        if k > 1:
            b_next[k - 1].wait_recv()
        src = woutb.at[zb(k - 1), x]
        b_next[k] = send(src, src, z_next)
        if k <= 3:
            if k > 1:
                b_prev[k - 1].wait_recv()
            src = woutb.at[zb(1 - k), x]
            b_prev[k] = send(src, src, z_prev)

    a_step(1, 0)
    b_step(1)
    b_cross(0)

    arrive(reqs1)
    for zz in range(NZ):
        tile = rcv1[zz]
        mine = jnp.where(iota((16, 128), 0) == z, tile, 0.0)
        req2[zz : zz + 1, :] = jnp.sum(mine, axis=0, keepdims=True)
        req2[NZ + zz : NZ + zz + 1, :] = tile[NZ : NZ + 1, :]
    rcv2[p] = req2[...]
    reqs2 = [send(req2, rcv2.at[p], p_peer(o)) for o in range(1, NP)]

    for j in range(1, NX):
        a_step(1, j)
    b_step(2)
    b_cross(1)
    b_cross(-1)
    b_relay(0)

    arrive(reqs2)
    asked = jnp.concatenate([rcv2[pp, 0:NZ, :] for pp in range(NP)], axis=0).astype(BF)
    slots = NZ * NP * CAP
    thrice = dot(bits((iota((slots, NZ * NP), 0) >> 2) == iota((slots, NZ * NP), 1)), asked)
    lane_mine = iota((slots, 128), 1) == (iota((slots, 128), 0) & (CAP - 1)) + CAP * p
    wanted = jnp.sum(jnp.where(lane_mine, thrice, 0.0), axis=1, keepdims=True).astype(I32)
    pick = bits(wanted == iota((slots, table.shape[0]), 1))
    g1b[...] = dot(pick, table[...]).astype(BF).reshape(g1b.shape)
    ra[p] = g1b[p]
    rows1 = [send(g1b.at[lax.rem(p + o, NP)], ra.at[p], p_peer(o)) for o in range(1, NP)]

    for j in range(NX):
        a_step(2, j)
    b_step(3)
    b_cross(2)
    b_cross(-2)
    b_relay(1)
    b_relay(-1)

    arrive(rows1)
    i0 = iota((slots, slots), 0)
    order1 = ((i0 >> 2) & (NP - 1)) * 32 + (i0 >> 5) * CAP + (i0 & (CAP - 1))
    regrouped = dot(bits(order1 == iota((slots, slots), 1)), ra[...].reshape(slots, -1))
    bb[...] = regrouped.astype(BF).reshape(bb.shape)
    fb[z] = bb[z]
    rows2 = [send(bb.at[lax.rem(z + o, NZ)], fb.at[z], z_peer(o)) for o in range(1, NZ)]

    for j in range(NX):
        a_step(3, j)
    b_step(4)
    b_prev[3].wait_recv()
    b_cross(3)
    b_cross(-3)
    b_relay(2)
    b_relay(-2)
    arrive(tool_sends)
    for o in range(1, NYH):
        slot = toolsb.at[c * NYH + lax.rem(yh + o, NYH)]
        tool_swaps.append(send(slot, slot, other_core))

    arrive(rows2)
    select = bits(owner * CAP + rank == iota((chains, slots), 1))
    combined = queries[...].astype(F32) + dot(select, fb[...].reshape(slots, -1))
    centred = combined - jnp.mean(combined, axis=1, keepdims=True)
    spread_sq = jnp.mean(centred * centred, axis=1, keepdims=True)
    normed = centred * lax.rsqrt(spread_sq + 1e-05) * gain[...].astype(F32)
    nbuf[c] = normed.astype(BF)
    swap_n = send(nbuf.at[c], nbuf.at[c], other_core)

    for j in range(NX):
        a_step(4, j)
    b_next[4].wait_recv()
    b_cross(4)
    b_relay(3)
    b_relay(-3)
    b_relay(4)

    units = w_in.shape[0]
    hidden = NZ * NX * units
    bias_rows = jnp.concatenate([rcv2[NYL * xx + c, NZ : 2 * NZ, :] for xx in range(NX)], axis=0)
    lane = iota((128, hidden), 1)
    spread_bias = dot(bias_rows.astype(BF), bits(iota((128, hidden), 0) == lane - units * ((lane * 1366) >> 16)))
    shard = (iota((NX * NZ, hidden), 1) * 1366) >> 16
    shard_row = (shard & (NX - 1)) * NZ + (shard >> 2)
    bias_row = jnp.sum(jnp.where(shard_row == iota((NX * NZ, hidden), 0), spread_bias, 0.0), axis=0, keepdims=True)

    swap_n.wait_recv()
    for j in range(NX):
        a_prev[3, j].wait_recv()
        a_next[4, j].wait_recv()
    for k in (0, 1, -1, 2, -2, 3, -3, 4):
        b_x[k, -1].wait_recv()
        b_x[k, 2].wait_recv()

    both = nbuf[...].reshape(2 * chains, -1)
    group = 2
    width = group * NX * units
    branch = None
    for g in range(NZ // group):
        block = winb[g * group : (g + 1) * group].reshape(width, -1)
        act = gelu(dot_t(both, block) + bias_row[:, g * width : (g + 1) * width]).astype(BF)
        term = dot(act, woutb[g * group : (g + 1) * group].reshape(width, -1))
        branch = term if branch is None else branch + term
    pbuf[...] = branch.reshape(pbuf.shape)
    swap_p = send(pbuf.at[1 - c], rbuf, other_core)
    swap_p.wait_recv()
    updated = (combined + (pbuf[c] + rbuf[...]) + bias_out[...].astype(F32)).astype(BF)
    updated_ref[...] = updated
    updb[c] = updated
    swap_u = send(updb.at[c], updb.at[c], other_core)

    arrive(tool_swaps)
    own_tools.wait()
    all_tools = toolsb[...].reshape(NC * NYH * tools.shape[0], -1)
    n_tools = all_tools.shape[0]
    half = n_tools // 2
    scores = dot_t(updated, all_tools)
    pos = jnp.sum(jnp.where(eye, positive[...].astype(F32), 0.0), axis=1, keepdims=True).astype(I32)
    pos_col = ((pos >> 6) & 1) * half + (pos >> 7) * 64 + (pos & 63)
    is_pos = iota((chains, n_tools), 1) == pos_col
    top = jnp.max(scores, axis=1, keepdims=True)
    log_total = top + jnp.log(jnp.sum(jnp.exp(scores - top), axis=1, keepdims=True))
    loss = log_total - jnp.sum(jnp.where(is_pos, scores, 0.0), axis=1, keepdims=True)
    grad = (jnp.exp(scores - log_total) - jnp.where(is_pos, 1.0, 0.0)).astype(BF)
    wgb[0] = grad[:, :half]
    wgb[1] = grad[:, half:]
    swap_w = send(wgb.at[1 - c], wga.at[c], other_core)
    wga[c] = wgb[c]
    loss_ref[...] = jnp.sum(jnp.where(eye, loss, 0.0), axis=0, keepdims=True)
    qgrad_ref[...] = dot(grad, all_tools)

    arrive([swap_u, swap_w])
    i1 = iota((half, half), 0)
    order2 = ((i1 >> 3) & (NYH - 1)) * 64 + (i1 >> 5) * 8 + (i1 & 7)
    grad_t = dot_t(bits(order2 == iota((half, half), 1)), wga[...].reshape(2 * chains, half)).astype(BF)
    part = dot(grad_t, updb[...].reshape(2 * chains, -1))
    s1b[...] = part.astype(BF).reshape(s1b.shape)
    s1r[p] = s1b[p]
    arrive([send(s1b.at[lax.rem(p + o, NP)], s1r.at[p], p_peer(o)) for o in range(1, NP)])
    total = s1r[0].astype(F32)
    for i in range(1, NP):
        total = total + s1r[i].astype(F32)
    s2b[...] = total.reshape(s2b.shape)
    s2r[yh] = s2b[yh]
    arrive([send(s2b.at[lax.rem(yh + o, NYH)], s2r.at[yh], y_peer(o)) for o in range(1, NYH)])
    total = s2r[0]
    for i in range(1, NYH):
        total = total + s2r[i]
    s3b[...] = total
    s3r[z] = total
    arrive([send(s3b, s3r.at[z], z_peer(o)) for o in range(1, NZ)])
    total = s3r[0]
    for i in range(1, NZ):
        total = total + s3r[i]
    s4r[p] = total * grad_scale
    arrive([send(s4r.at[p], s4r.at[p], p_peer(o)) for o in range(1, NP)])
    tgrad_ref[...] = s4r[...].reshape(tgrad_ref.shape)

    for copy in started:
        copy.wait_send()

    @pl.when(c == yl)
    def _():
        y_in.wait_send()
        y_out.wait_send()


def solution(mesh):
    def local(queries, owner, row, table, gain, w_in, bias_in, w_out, bias_out, tools, positive):
        n, feat = queries.shape
        units = w_in.shape[0]
        block = tools.shape[0]
        scale = (block * mesh.shape["dp"] / (n * mesh.shape["dp"] * mesh.shape["mp"])) ** 0.5
        vmem = pl.BlockSpec(memory_space=pltpu.VMEM)
        slot_rows = NP * CAP
        sub = block // NP
        scratch = [
            pltpu.VMEM((NZ, NX, units, feat), BF),
            pltpu.VMEM((NZ, NX, units, feat), BF),
            pltpu.VMEM((NC * NYH, block, feat), BF),
            pltpu.VMEM((16, 128), F32),
            pltpu.VMEM((NZ, 16, 128), F32),
            pltpu.VMEM((16, 128), F32),
            pltpu.VMEM((NP, 16, 128), F32),
            pltpu.VMEM((NP, slot_rows, feat), BF),
            pltpu.VMEM((NP, slot_rows, feat), BF),
            pltpu.VMEM((NZ, slot_rows, feat), BF),
            pltpu.VMEM((NZ, slot_rows, feat), BF),
            pltpu.VMEM((NC, n, feat), BF),
            pltpu.VMEM((NC, n, feat), F32),
            pltpu.VMEM((n, feat), F32),
            pltpu.VMEM((NC, n, feat), BF),
            pltpu.VMEM((NC, n, NYH * block), BF),
            pltpu.VMEM((NC, n, NYH * block), BF),
            pltpu.VMEM((NP, NYH * sub, feat), BF),
            pltpu.VMEM((NP, NYH * sub, feat), BF),
            pltpu.VMEM((NYH, sub, feat), F32),
            pltpu.VMEM((NYH, sub, feat), F32),
            pltpu.VMEM((sub, feat), F32),
            pltpu.VMEM((NZ, sub, feat), F32),
            pltpu.VMEM((NP, sub, feat), F32),
            pltpu.SemaphoreType.DMA((N_SEMS,)),
            pltpu.SemaphoreType.DMA((N_SEMS,)),
            pltpu.SemaphoreType.DMA((3,)),
        ]
        updated, loss, qgrad, tgrad = pl.pallas_call(
            functools.partial(kernel, scale),
            out_shape=(
                jax.ShapeDtypeStruct((n, feat), BF),
                jax.ShapeDtypeStruct((1, n), F32),
                jax.ShapeDtypeStruct((n, feat), F32),
                jax.ShapeDtypeStruct((block, feat), F32),
            ),
            in_specs=[vmem] * 11,
            out_specs=(vmem,) * 4,
            scratch_shapes=scratch,
            compiler_params=pltpu.CompilerParams(
                collective_id=0, has_side_effects=True, vmem_limit_bytes=48 << 20
            ),
        )(
            queries,
            owner,
            row.reshape(1, n),
            table,
            gain.reshape(1, feat),
            w_in,
            jnp.pad(bias_in.reshape(1, units), ((0, 0), (0, 128 - units))),
            w_out,
            bias_out.reshape(1, feat),
            tools,
            positive.reshape(1, n),
        )
        return updated, loss.reshape(n), qgrad, tgrad

    in_specs = (
        P(("dp", "mp"), None),
        P(("dp", "mp"), None),
        P(("dp", "mp")),
        P("mp", None),
        P(),
        P("mp", None),
        P("mp"),
        P("mp", None),
        P(),
        P("dp", None),
        P(("dp", "mp")),
    )
    out_specs = (P(("dp", "mp"), None), P(("dp", "mp")), P(("dp", "mp"), None), P("dp", None))
    return jax.shard_map(local, mesh=mesh, in_specs=in_specs, out_specs=out_specs, check_vma=False)
```

time: 1270 us -> 104 us (0.08)
  the two profiles are of different devices: /device:TPU:2 before, /device:TPU:8 now
where the time goes in v1:
time: 104 us
  Pallas kernels  94.2 us (91%)
  local copies, waits for them, and re-layouts  9.17 us (9%)
    pallas_call x1, Pallas kernels, local(): pl.pallas_call(functools.partial(kernel, scale), out_shape=(jax.ShapeDtyp...  94.2 us
    unnamed x19, local copies, waits for them, and re-layouts  7.1 us

profile of v1, /device:TPU:8, one launch (start us, length us, event | category | flops | bytes accessed | tf_op | source)
XLA Modules:
  0.0 104.1 jit_solution(10189063360087268736)
XLA Ops:
  0.6 0.0 copy-start.3
  0.6 0.7 pad.4.bias_in
  1.3 0.7 reshape.27.gain
  2.0 0.7 reshape.29.bias_out
  2.7 0.0 copy-start.5
  2.7 0.0 copy-start.6
  2.7 0.8 copy.15.owner_ref
  3.5 0.0 copy-done.3
  3.5 0.0 copy-done.5
  3.5 0.0 copy-done.6
  3.5 0.0 copy-start
  3.5 1.0 copy-done
  4.5 0.0 copy-start.1
  4.5 0.9 copy-done.1
  5.5 0.0 copy-start.2
  5.5 0.9 copy-done.2
  6.3 0.0 copy-start.4
  6.3 0.9 copy-done.4
  7.2 94.2 %shard_map.138 = (bf16[128,768]{1,0:T(8,128)(2,1)S(1)}, f32[1,128]{1,0:T(1,128)S(1)}, f32[128,768]{1,0:T(8,128)S(1)}, f32[64,768]{1,0:T(8,128)S(1)}) custom-call(bf16[128,768]{1,0:T(8,128)(2,1)S(1)} %copy-done.1, s32[128,1]{1,0:T(8,128)S(1)} %copy.15.owner_ref, s32[1,128]{1,0:T(1,128)S(1)} %bitcast.4, bf16[256,768]{1,0:T(8,128)(2,1)S(1)} %copy-done, ...), custom_call_target="tpu_custom_call" | custom-call | tf_op jit(solution)/shard_map/pallas_call | solution.py:432
  101.5 0.7 copy.20
  102.1 0.5 copy.21
  102.7 0.7 copy.22
  103.4 0.7 copy.23
Async XLA Ops:
  0.6 2.9 %copy-start.3 = (bf16[48,768]{1,0:T(8,128)(2,1)S(1)}, bf16[48,768]{1,0:T(8,128)(2,1)}, u32[]{:S(2)}) copy-start(bf16[48,768]{1,0:T(8,128)(2,1)} %w_in.1) | copy-start | bytes 221188
  2.7 0.8 copy-start.5
  2.7 0.8 copy-start.6
  3.5 1.0 copy-start
  4.5 0.9 copy-start.1
  5.5 0.9 copy-start.2
  6.3 0.9 copy-start.4

commit v2 on v1

v2 whole, which is shorter than its diff:
```python
import functools

import jax
import jax.numpy as jnp
from jax import lax
from jax.experimental import pallas as pl
from jax.experimental.pallas import tpu as pltpu
from jax.sharding import PartitionSpec as P

MESH = pl.DeviceIdType.MESH
BF, F32, I32 = jnp.bfloat16, jnp.float32, jnp.int32
NZ, NX, NYL, NYH, NC = 8, 4, 2, 4, 2
NP = NX * NYL
CAP = 4
N_SEMS = 192


def iota(shape, axis):
    return lax.broadcasted_iota(I32, shape, axis)


def bits(mask):
    return jnp.where(mask, 1.0, 0.0).astype(BF)


def dot(a, b):
    return jnp.dot(a, b, preferred_element_type=F32)


def dot_t(a, b):
    return lax.dot_general(a, b, (((1,), (1,)), ((), ())), preferred_element_type=F32)


def gelu(u):
    return 0.5 * u * (1.0 + jnp.tanh(0.7978845608028654 * (u + 0.044715 * (u * u * u))))


def kernel(
    grad_scale,
    queries_hbm,
    owner_hbm,
    row_hbm,
    positive_hbm,
    table_hbm,
    w_in,
    w_out,
    tools,
    gain_hbm,
    bias_out_hbm,
    bias_in_hbm,
    updated_ref,
    loss_ref,
    qgrad_ref,
    tgrad_ref,
    queries,
    owner_ref,
    row_ref,
    positive,
    table,
    gain_ref,
    bias_out_ref,
    bias_in_ref,
    bias_mat,
    wb,
    toolsb,
    req1,
    rcv1,
    req2,
    rcv2,
    g1b,
    ra,
    bb,
    fb,
    nbuf,
    pbuf,
    rbuf,
    updb,
    wgb,
    wga,
    s1b,
    s1r,
    s2b,
    s2r,
    s3b,
    s3r,
    s4r,
    send_sems,
    recv_sems,
    local_sems,
):
    d, m = lax.axis_index("dp"), lax.axis_index("mp")
    yh, c = lax.div(d, NC), lax.rem(d, NC)
    z, p = lax.div(m, NP), lax.rem(m, NP)
    x, yl = lax.div(p, NYL), lax.rem(p, NYL)
    chains, feat = queries.shape
    units = w_in.shape[0]
    split = 2 * units // 3

    def z_peer(o):
        return {"mp": lax.rem(z + o, NZ) * NP + p}

    def p_peer(o):
        return {"mp": z * NP + lax.rem(p + o, NP)}

    def x_peer(o):
        return {"mp": z * NP + lax.rem(x + o, NX) * NYL + yl}

    def y_peer(o):
        return {"dp": lax.rem(yh + o, NYH) * NC + c}

    other_core = {"dp": yh * NC + (1 - c)}
    y_flip = {"mp": z * NP + x * NYL + (1 - yl)}
    z_next = {"mp": lax.rem(z + 1 + (NZ - 2) * c, NZ) * NP + p}
    z_prev = {"mp": lax.rem(z + (NZ - 1) - (NZ - 2) * c, NZ) * NP + p}
    x_next = {"mp": z * NP + lax.rem(x + 1 + (NX - 2) * c, NX) * NYL + yl}
    x_prev = {"mp": z * NP + lax.rem(x + (NX - 1) - (NX - 2) * c, NX) * NYL + yl}

    def zb(k):
        return lax.rem(z - k + 2 * k * c + NZ, NZ)

    def xb(k):
        return lax.rem(x - k + 2 * k * c + NX, NX)

    count = [0]
    started = []
    arrived = set()

    def remote(src, dst, peer):
        i = count[0]
        count[0] += 1
        return pltpu.make_async_remote_copy(
            src_ref=src,
            dst_ref=dst,
            send_sem=send_sems.at[i],
            recv_sem=recv_sems.at[i],
            device_id=peer,
            device_id_type=MESH,
        )

    def send(src, dst, peer):
        copy = remote(src, dst, peer)
        copy.start()
        started.append(copy)
        return copy

    def arrive(copies):
        for copy in copies:
            if id(copy) not in arrived:
                arrived.add(id(copy))
                copy.wait_recv()

    barrier = pltpu.get_barrier_semaphore()
    peers = [z_peer(o) for o in range(1, NZ)] + [p_peer(o) for o in range(1, NP)]
    peers += [y_peer(o) for o in range(1, NYH)] + [other_core]
    for peer in peers:
        pl.semaphore_signal(barrier, inc=1, device_id=peer, device_id_type=MESH)

    def load(src, dst, i):
        copy = pltpu.make_async_copy(src, dst, local_sems.at[i])
        copy.start()
        return copy

    smalls = [
        (owner_hbm, owner_ref),
        (row_hbm, row_ref),
        (positive_hbm, positive),
        (gain_hbm, gain_ref),
        (bias_out_hbm, bias_out_ref),
        (bias_in_hbm, bias_in_ref),
    ]
    small_loads = [load(src, dst, 7 + i) for i, (src, dst) in enumerate(smalls)]
    table_load = load(table_hbm, table, 2)
    queries_load = load(queries_hbm, queries, 3)
    own_tools = load(tools, toolsb.at[c * NYH + yh], 4)
    for copy in small_loads:
        copy.wait()
    gain = gain_ref[...].astype(F32).reshape(1, feat)
    bias_out = bias_out_ref[...].astype(F32).reshape(1, feat)
    bias_in = jnp.pad(bias_in_ref[...].astype(F32).reshape(1, units), ((0, 0), (0, 128 - units)))

    eye = iota((chains, chains), 0) == iota((chains, chains), 1)
    owner_row = owner_ref[...]
    owner = jnp.sum(jnp.where(eye, owner_row.astype(F32), 0.0), axis=1, keepdims=True).astype(I32)
    own_mask = owner == iota((chains, NZ * NP), 1)
    earlier = bits(iota((chains, chains), 1) < iota((chains, chains), 0))
    prior = dot(earlier, bits(own_mask))
    rank = jnp.sum(jnp.where(own_mask, prior, 0.0), axis=1, keepdims=True).astype(I32)
    row_col = jnp.sum(jnp.where(eye, row_ref[...].astype(F32), 0.0), axis=1, keepdims=True)
    lane_of = (owner & (NP - 1)) * CAP + rank
    spread = jnp.where(iota((chains, 128), 1) == lane_of, row_col, 0.0).astype(BF)
    to_z = bits((owner_row >> 3) == iota((16, chains), 0))
    bias_line = jnp.where(iota((16, 128), 0) == NZ, bias_in, 0.0)
    req1[...] = dot(to_z, spread) + bias_line
    rcv1[z] = req1[...]
    pl.semaphore_wait(barrier, len(peers))
    reqs1 = [send(req1, rcv1.at[z], z_peer(o)) for o in range(1, NZ)]

    in_slot, out_slot = wb.at[z, x, 0:units], wb.at[z, x, units : 2 * units]
    y_in = remote(w_in, in_slot, y_flip)
    y_out = remote(w_out, out_slot, y_flip)
    own_in = pltpu.make_async_copy(w_in, in_slot, local_sems.at[5])
    own_out = pltpu.make_async_copy(w_out, out_slot, local_sems.at[6])

    @pl.when(c == yl)
    def _():
        y_in.start()
        y_out.start()
        own_in.start()
        own_out.start()

    @pl.when(c == yl)
    def _():
        own_in.wait()
        own_out.wait()

    @pl.when(c != yl)
    def _():
        y_in.wait_recv()
        y_out.wait_recv()

    def a_part(zz, xx):
        return wb.at[zz, xx, 0:split]

    def b_part(zz, xx):
        return wb.at[zz, xx, split : 2 * units]

    a_x = {NX - o: send(a_part(z, x), a_part(z, x), x_peer(o)) for o in range(1, NX)}
    a_next, a_prev, b_next, b_prev, b_x = {}, {}, {}, {}, {}

    def a_step(k, j):
        xj = lax.rem(x + j, NX)
        if k == 1 and j > 0:
            arrive([a_x[j]])
        if k > 1:
            arrive([a_next[k - 1, j]])
        src = a_part(zb(k - 1), xj)
        a_next[k, j] = send(src, src, z_next)
        if k <= 3:
            if k > 1:
                arrive([a_prev[k - 1, j]])
            src = a_part(zb(1 - k), xj)
            a_prev[k, j] = send(src, src, z_prev)

    def b_cross(k):
        if k:
            arrive([b_next[k] if k > 0 else b_prev[-k]])
        src = b_part(zb(k), x)
        b_x[k, 1] = send(src, src, x_next)
        b_x[k, -1] = send(src, src, x_prev)

    def b_relay(k):
        arrive([b_x[k, 1]])
        src = b_part(zb(k), xb(1))
        b_x[k, 2] = send(src, src, x_next)

    def b_step(k):
        if k > 1:
            arrive([b_next[k - 1]])
        src = b_part(zb(k - 1), x)
        b_next[k] = send(src, src, z_next)
        if k <= 3:
            if k > 1:
                arrive([b_prev[k - 1]])
            src = b_part(zb(1 - k), x)
            b_prev[k] = send(src, src, z_prev)

    b_step(1)
    a_step(1, 0)
    b_cross(0)

    arrive(reqs1)
    for zz in range(NZ):
        tile = rcv1[zz]
        mine = jnp.where(iota((16, 128), 0) == z, tile, 0.0)
        req2[zz : zz + 1, :] = jnp.sum(mine, axis=0, keepdims=True)
        req2[NZ + zz : NZ + zz + 1, :] = tile[NZ : NZ + 1, :]
    rcv2[p] = req2[...]
    reqs2 = [send(req2, rcv2.at[p], p_peer(o)) for o in range(1, NP)]

    b_step(2)
    b_cross(1)
    b_cross(-1)
    for j in range(1, NX):
        a_step(1, j)
    b_relay(0)

    arrive(reqs2)
    table_load.wait()
    asked = jnp.concatenate([rcv2[pp, 0:NZ, :] for pp in range(NP)], axis=0).astype(BF)
    slots = NZ * NP * CAP
    thrice = dot(bits((iota((slots, NZ * NP), 0) >> 2) == iota((slots, NZ * NP), 1)), asked)
    lane_mine = iota((slots, 128), 1) == (iota((slots, 128), 0) & (CAP - 1)) + CAP * p
    wanted = jnp.sum(jnp.where(lane_mine, thrice, 0.0), axis=1, keepdims=True).astype(I32)
    pick = bits(wanted == iota((slots, table.shape[0]), 1))
    g1b[...] = dot(pick, table[...]).astype(BF).reshape(g1b.shape)
    ra[p] = g1b[p]
    rows1 = [send(g1b.at[lax.rem(p + o, NP)], ra.at[p], p_peer(o)) for o in range(1, NP)]

    b_step(3)
    b_cross(2)
    b_cross(-2)
    a_step(2, 0)
    a_step(2, 1)
    b_relay(1)
    b_relay(-1)

    arrive(rows1)
    i0 = iota((slots, slots), 0)
    order1 = ((i0 >> 2) & (NP - 1)) * 32 + (i0 >> 5) * CAP + (i0 & (CAP - 1))
    regrouped = dot(bits(order1 == iota((slots, slots), 1)), ra[...].reshape(slots, -1))
    bb[...] = regrouped.astype(BF).reshape(bb.shape)
    fb[z] = bb[z]
    tool_sends = [send(tools, toolsb.at[c * NYH + yh], y_peer(o)) for o in range(1, NYH)]
    tool_swaps = [send(tools, toolsb.at[c * NYH + yh], other_core)]
    rows2 = [send(bb.at[lax.rem(z + o, NZ)], fb.at[z], z_peer(o)) for o in range(1, NZ)]

    b_step(4)
    b_cross(3)
    b_cross(-3)
    a_step(2, 2)
    a_step(2, 3)
    b_relay(2)
    b_relay(-2)
    b_cross(4)
    a_step(3, 0)
    a_step(3, 1)
    b_relay(3)
    b_relay(-3)

    width = NX * units
    bias_rows = jnp.concatenate([rcv2[NYL * xx + c, NZ : 2 * NZ, :] for xx in range(NX)], axis=1)
    line = iota((NX * 128, width), 0)
    lane_to = bits(((line & 127) < units) & (iota((NX * 128, width), 1) == (line >> 7) * units + (line & 127)))
    bias_mat[...] = dot(bias_rows.astype(BF), lane_to)
    queries_load.wait()

    arrive(rows2)
    select = bits(owner * CAP + rank == iota((chains, slots), 1))
    combined = queries[...].astype(F32) + dot(select, fb[...].reshape(slots, -1))
    centred = combined - jnp.mean(combined, axis=1, keepdims=True)
    spread_sq = jnp.mean(centred * centred, axis=1, keepdims=True)
    normed = centred * lax.rsqrt(spread_sq + 1e-05) * gain
    nbuf[c] = normed.astype(BF)
    swap_n = send(nbuf.at[c], nbuf.at[c], other_core)

    a_step(3, 2)
    a_step(3, 3)
    b_relay(4)

    arrive([swap_n])
    both = nbuf[...].reshape(2 * chains, feat)

    def hidden(k):
        if k:
            arrive([(a_next if k > 0 else a_prev)[abs(k), j] for j in range(NX)])
        arrive([b_x[k, -1], b_x[k, 2]])
        zz = zb(k)
        pre = dot_t(both, wb[zz, :, 0:units].reshape(width, feat)) + bias_mat[pl.ds(zz, 1), :]
        term = dot(gelu(pre).astype(BF), wb[zz, :, units : 2 * units].reshape(width, feat)).reshape(pbuf.shape)
        pbuf[...] = term if k == 0 else pbuf[...] + term

    hidden(0)
    for j in range(NX):
        a_step(4, j)
    arrive(tool_sends)
    for o in range(1, NYH):
        slot = toolsb.at[c * NYH + lax.rem(yh + o, NYH)]
        tool_swaps.append(send(slot, slot, other_core))
    for k in (1, -1, 2, -2, 3, -3, 4):
        hidden(k)
    swap_p = send(pbuf.at[1 - c], rbuf, other_core)
    arrive([swap_p])
    updated = (combined + (pbuf[c] + rbuf[...]) + bias_out).astype(BF)
    updated_ref[...] = updated
    updb[c] = updated
    swap_u = send(updb.at[c], updb.at[c], other_core)

    arrive(tool_swaps)
    own_tools.wait()
    all_tools = toolsb[...].reshape(NC * NYH * tools.shape[0], -1)
    n_tools = all_tools.shape[0]
    half = n_tools // 2
    scores = dot_t(updated, all_tools)
    pos = jnp.sum(jnp.where(eye, positive[...].astype(F32), 0.0), axis=1, keepdims=True).astype(I32)
    pos_col = ((pos >> 6) & 1) * half + (pos >> 7) * 64 + (pos & 63)
    is_pos = iota((chains, n_tools), 1) == pos_col
    top = jnp.max(scores, axis=1, keepdims=True)
    log_total = top + jnp.log(jnp.sum(jnp.exp(scores - top), axis=1, keepdims=True))
    loss = log_total - jnp.sum(jnp.where(is_pos, scores, 0.0), axis=1, keepdims=True)
    grad = (jnp.exp(scores - log_total) - jnp.where(is_pos, 1.0, 0.0)).astype(BF)
    wgb[0] = grad[:, :half]
    wgb[1] = grad[:, half:]
    swap_w = send(wgb.at[1 - c], wga.at[c], other_core)
    wga[c] = wgb[c]

    arrive([swap_u, swap_w])
    i1 = iota((half, half), 0)
    order2 = ((i1 >> 3) & (NYH - 1)) * 64 + (i1 >> 5) * 8 + (i1 & 7)
    grad_t = dot_t(bits(order2 == iota((half, half), 1)), wga[...].reshape(2 * chains, half)).astype(BF)
    part = dot(grad_t, updb[...].reshape(2 * chains, -1))
    s1b[...] = part.astype(BF).reshape(s1b.shape)
    s1r[p] = s1b[p]
    stage1 = [send(s1b.at[lax.rem(p + o, NP)], s1r.at[p], p_peer(o)) for o in range(1, NP)]
    loss_ref[...] = jnp.sum(jnp.where(eye, loss, 0.0), axis=0, keepdims=True)
    qgrad_ref[...] = dot(grad, all_tools)
    arrive(stage1)
    total = s1r[0].astype(F32)
    for i in range(1, NP):
        total = total + s1r[i].astype(F32)
    s2b[...] = total.reshape(s2b.shape).astype(BF)
    s2r[yh] = s2b[yh]
    arrive([send(s2b.at[lax.rem(yh + o, NYH)], s2r.at[yh], y_peer(o)) for o in range(1, NYH)])
    total = s2r[0].astype(F32)
    for i in range(1, NYH):
        total = total + s2r[i].astype(F32)
    s3b[...] = total.astype(BF)
    s3r[z] = s3b[...]
    arrive([send(s3b, s3r.at[z], z_peer(o)) for o in range(1, NZ)])
    total = s3r[0].astype(F32)
    for i in range(1, NZ):
        total = total + s3r[i].astype(F32)
    s4r[p] = (total * grad_scale).astype(BF)
    arrive([send(s4r.at[p], s4r.at[p], p_peer(o)) for o in range(1, NP)])
    tgrad_ref[...] = s4r[...].astype(F32).reshape(tgrad_ref.shape)

    for copy in started:
        copy.wait_send()

    @pl.when(c == yl)
    def _():
        y_in.wait_send()
        y_out.wait_send()


def hand_over(*refs):
    sems = refs[8]
    copies = [pltpu.make_async_copy(refs[i], refs[4 + i], sems.at[i]) for i in range(4)]
    for copy in copies:
        copy.start()
    for copy in copies:
        copy.wait()


def solution(mesh):
    def local(queries, owner, row, table, gain, w_in, bias_in, w_out, bias_out, tools, positive):
        n, feat = queries.shape
        units = w_in.shape[0]
        block = tools.shape[0]
        scale = (block * mesh.shape["dp"] / (n * mesh.shape["dp"] * mesh.shape["mp"])) ** 0.5
        vmem = pl.BlockSpec(memory_space=pltpu.VMEM)
        slot_rows = NP * CAP
        sub = block // NP
        scratch = [
            pltpu.VMEM((n, feat), BF),
            pltpu.VMEM((1, n), I32),
            pltpu.VMEM((1, n), I32),
            pltpu.VMEM((1, n), I32),
            pltpu.VMEM(table.shape, BF),
            pltpu.VMEM((feat,), BF),
            pltpu.VMEM((feat,), BF),
            pltpu.VMEM((units,), BF),
            pltpu.VMEM((NZ, NX * units), F32),
            pltpu.VMEM((NZ, NX, 2 * units, feat), BF),
            pltpu.VMEM((NC * NYH, block, feat), BF),
            pltpu.VMEM((16, 128), F32),
            pltpu.VMEM((NZ, 16, 128), F32),
            pltpu.VMEM((16, 128), F32),
            pltpu.VMEM((NP, 16, 128), F32),
            pltpu.VMEM((NP, slot_rows, feat), BF),
            pltpu.VMEM((NP, slot_rows, feat), BF),
            pltpu.VMEM((NZ, slot_rows, feat), BF),
            pltpu.VMEM((NZ, slot_rows, feat), BF),
            pltpu.VMEM((NC, n, feat), BF),
            pltpu.VMEM((NC, n, feat), F32),
            pltpu.VMEM((n, feat), F32),
            pltpu.VMEM((NC, n, feat), BF),
            pltpu.VMEM((NC, n, NYH * block), BF),
            pltpu.VMEM((NC, n, NYH * block), BF),
            pltpu.VMEM((NP, NYH * sub, feat), BF),
            pltpu.VMEM((NP, NYH * sub, feat), BF),
            pltpu.VMEM((NYH, sub, feat), BF),
            pltpu.VMEM((NYH, sub, feat), BF),
            pltpu.VMEM((sub, feat), BF),
            pltpu.VMEM((NZ, sub, feat), BF),
            pltpu.VMEM((NP, sub, feat), BF),
            pltpu.SemaphoreType.DMA((N_SEMS,)),
            pltpu.SemaphoreType.DMA((N_SEMS,)),
            pltpu.SemaphoreType.DMA((13,)),
        ]
        updated, loss, qgrad, tgrad = pl.pallas_call(
            functools.partial(kernel, scale),
            out_shape=(
                jax.ShapeDtypeStruct((n, feat), BF),
                jax.ShapeDtypeStruct((1, n), F32),
                jax.ShapeDtypeStruct((n, feat), F32),
                jax.ShapeDtypeStruct((block, feat), F32),
            ),
            in_specs=[pl.BlockSpec(memory_space=pltpu.HBM)] * 11,
            out_specs=(vmem,) * 4,
            scratch_shapes=scratch,
            compiler_params=pltpu.CompilerParams(
                collective_id=0, has_side_effects=True, vmem_limit_bytes=63 << 20
            ),
        )(
            queries,
            owner.reshape(1, n),
            row.reshape(1, n),
            positive.reshape(1, n),
            table,
            w_in,
            w_out,
            tools,
            gain,
            bias_out,
            bias_in,
        )
        results = (updated, loss, qgrad, tgrad)
        hbm = pl.BlockSpec(memory_space=pltpu.HBM)
        updated, loss, qgrad, tgrad = pl.pallas_call(
            hand_over,
            out_shape=tuple(jax.ShapeDtypeStruct(r.shape, r.dtype) for r in results),
            in_specs=[hbm] * 4,
            out_specs=(hbm,) * 4,
            scratch_shapes=[pltpu.SemaphoreType.DMA((4,))],
            compiler_params=pltpu.CompilerParams(vmem_limit_bytes=63 << 20),
        )(*results)
        return updated, loss.reshape(n), qgrad, tgrad

    in_specs = (
        P(("dp", "mp"), None),
        P(("dp", "mp"), None),
        P(("dp", "mp")),
        P("mp", None),
        P(),
        P("mp", None),
        P("mp"),
        P("mp", None),
        P(),
        P("dp", None),
        P(("dp", "mp")),
    )
    out_specs = (P(("dp", "mp"), None), P(("dp", "mp")), P(("dp", "mp"), None), P("dp", None))
    return jax.shard_map(local, mesh=mesh, in_specs=in_specs, out_specs=out_specs, check_vma=False)
```

time: 104 us -> 112 us (1.077)
  the two profiles are of different devices: /device:TPU:8 before, /device:TPU:2 now
where the time goes in v2:
time: 112 us; the launch traced here: 111 us
  Pallas kernels  111 us (99%)
    pallas_call x1, Pallas kernels, local(): pl.pallas_call(functools.partial(kernel, scale), out_shape=(jax.ShapeDtyp...  85.8 us
    pallas_call x1, Pallas kernels, local(): pl.pallas_call(hand_over, out_shape=tuple((jax.ShapeDtypeStruct(r.shape,...  25 us

profile of v2, /device:TPU:2, one launch (start us, length us, event | category | flops | bytes accessed | tf_op | source)
XLA Modules:
  0.0 111.5 jit_solution(8953278346092012076)
XLA Ops:
  0.6 85.8 %shard_map.138 = (bf16[128,768]{1,0:T(8,128)(2,1)}, f32[1,128]{1,0:T(1,128)}, f32[128,768]{1,0:T(8,128)}, f32[64,768]{1,0:T(8,128)}) custom-call(bf16[128,768]{1,0:T(8,128)(2,1)} %queries_hbm.1, s32[1,128]{1,0:T(1,128)} %bitcast.4, s32[1,128]{1,0:T(1,128)} %bitcast.5, s32[1,128]{1,0:T(1,128)} %bitcast.6, bf16[256,768]{1,0:T(8,128)(2,1)} %table_hbm.1, ...), custom_call_target="tpu_custom_call" | custom-call | tf_op jit(solution)/shard_map/pallas_call | solution.py:490
  86.5 25.0 %shard_map.139 = (bf16[128,768]{1,0:T(8,128)(2,1)}, f32[1,128]{1,0:T(1,128)}, f32[128,768]{1,0:T(8,128)}, f32[64,768]{1,0:T(8,128)}) custom-call(bf16[128,768]{1,0:T(8,128)(2,1)} %get-tuple-element.12.refs_0_, f32[1,128]{1,0:T(1,128)} %get-tuple-element.13.refs_1_, f32[128,768]{1,0:T(8,128)} %get-tuple-element.14.refs_2_, f32[64,768]{1,0:T(8,128)} %get-tuple-element.15.refs_3_), custom_call_target="tpu_custom_call" | custom-call | tf_op jit(solution)/shard_map/pallas_call | solution.py:519

commit v3 on v2

--- a/solution.py
+++ b/solution.py
@@ -433,11 +433,15 @@
 
 
 def hand_over(*refs):
-    sems = refs[8]
-    copies = [pltpu.make_async_copy(refs[i], refs[4 + i], sems.at[i]) for i in range(4)]
-    for copy in copies:
+    held, sems = refs[8:12], refs[12]
+    copies_in = [pltpu.make_async_copy(refs[i], held[i], sems.at[i]) for i in range(4)]
+    copies_out = [pltpu.make_async_copy(held[i], refs[4 + i], sems.at[4 + i]) for i in range(4)]
+    for copy in copies_in:
         copy.start()
-    for copy in copies:
+    for copy_in, copy_out in zip(copies_in, copies_out):
+        copy_in.wait()
+        copy_out.start()
+    for copy in copies_out:
         copy.wait()
 
 
@@ -521,7 +525,7 @@
             out_shape=tuple(jax.ShapeDtypeStruct(r.shape, r.dtype) for r in results),
             in_specs=[hbm] * 4,
             out_specs=(hbm,) * 4,
-            scratch_shapes=[pltpu.SemaphoreType.DMA((4,))],
+            scratch_shapes=[pltpu.VMEM(r.shape, r.dtype) for r in results] + [pltpu.SemaphoreType.DMA((8,))],
             compiler_params=pltpu.CompilerParams(vmem_limit_bytes=63 << 20),
         )(*results)
         return updated, loss.reshape(n), qgrad, tgrad

time: 112 us -> 88.7 us (0.79)
  Pallas kernels: 111 us -> 87.8 us
    pallas_call x1, Pallas kernels: 25 us -> 1.98 us  [local(): pl.pallas_call(hand_over, out_shape=tuple((jax.ShapeDtypeStruct(r.shape,...]
where the time goes in v3:
time: 88.7 us; the launch traced here: 88.5 us
  Pallas kernels  87.8 us (99%)
    pallas_call x1, Pallas kernels, local(): pl.pallas_call(functools.partial(kernel, scale), out_shape=(jax.ShapeDtyp...  85.8 us
    pallas_call x1, Pallas kernels, local(): pl.pallas_call(hand_over, out_shape=tuple((jax.ShapeDtypeStruct(r.shape,...  1.98 us

profile of v3, /device:TPU:2, one launch (start us, length us, event | category | flops | bytes accessed | tf_op | source)
XLA Modules:
  0.0 88.5 jit_solution(16273895108247080816)
XLA Ops:
  0.6 85.8 %shard_map.138 = (bf16[128,768]{1,0:T(8,128)(2,1)}, f32[1,128]{1,0:T(1,128)}, f32[128,768]{1,0:T(8,128)}, f32[64,768]{1,0:T(8,128)}) custom-call(bf16[128,768]{1,0:T(8,128)(2,1)} %queries_hbm.1, s32[1,128]{1,0:T(1,128)} %bitcast.4, s32[1,128]{1,0:T(1,128)} %bitcast.5, s32[1,128]{1,0:T(1,128)} %bitcast.6, bf16[256,768]{1,0:T(8,128)(2,1)} %table_hbm.1, ...), custom_call_target="tpu_custom_call" | custom-call | tf_op jit(solution)/shard_map/pallas_call | solution.py:494
  86.5 2.0 %shard_map.139 = (bf16[128,768]{1,0:T(8,128)(2,1)}, f32[1,128]{1,0:T(1,128)}, f32[128,768]{1,0:T(8,128)}, f32[64,768]{1,0:T(8,128)}) custom-call(bf16[128,768]{1,0:T(8,128)(2,1)} %get-tuple-element.12.refs_0_, f32[1,128]{1,0:T(1,128)} %get-tuple-element.13.refs_1_, f32[128,768]{1,0:T(8,128)} %get-tuple-element.14.refs_2_, f32[64,768]{1,0:T(8,128)} %get-tuple-element.15.refs_3_), custom_call_target="tpu_custom_call" | custom-call | tf_op jit(solution)/shard_map/pallas_call | solution.py:523

commit v4 on v3

--- a/solution.py
+++ b/solution.py
@@ -48,9 +48,9 @@
     gain_hbm,
     bias_out_hbm,
     bias_in_hbm,
-    updated_ref,
+    updated_hbm,
     loss_ref,
-    qgrad_ref,
+    qgrad_hbm,
     tgrad_ref,
     queries,
     owner_ref,
@@ -81,9 +81,9 @@
     s1r,
     s2b,
     s2r,
-    s3b,
     s3r,
     s4r,
+    qgrad_buf,
     send_sems,
     recv_sems,
     local_sems,
@@ -148,6 +148,20 @@
             if id(copy) not in arrived:
                 arrived.add(id(copy))
                 copy.wait_recv()
+
+    halves = range(2)
+    half_feat = feat // 2
+    cuts = [slice(h * half_feat, (h + 1) * half_feat) for h in halves]
+
+    def spread_out(buf, got, me, count, peer_of):
+        got[me] = buf[me]
+        return [send(buf.at[lax.rem(me + o, count)], got.at[me], peer_of(o)) for o in range(1, count)]
+
+    def added(got, count):
+        total = got[0].astype(F32)
+        for i in range(1, count):
+            total = total + got[i].astype(F32)
+        return total
 
     barrier = pltpu.get_barrier_semaphore()
     peers = [z_peer(o) for o in range(1, NZ)] + [p_peer(o) for o in range(1, NP)]
@@ -292,9 +306,10 @@
     lane_mine = iota((slots, 128), 1) == (iota((slots, 128), 0) & (CAP - 1)) + CAP * p
     wanted = jnp.sum(jnp.where(lane_mine, thrice, 0.0), axis=1, keepdims=True).astype(I32)
     pick = bits(wanted == iota((slots, table.shape[0]), 1))
-    g1b[...] = dot(pick, table[...]).astype(BF).reshape(g1b.shape)
-    ra[p] = g1b[p]
-    rows1 = [send(g1b.at[lax.rem(p + o, NP)], ra.at[p], p_peer(o)) for o in range(1, NP)]
+    rows1, rows2 = [], []
+    for h in halves:
+        g1b[h] = dot(pick, table[:, cuts[h]]).astype(BF).reshape(g1b.shape[1:])
+        rows1.append(spread_out(g1b.at[h], ra.at[h], p, NP, p_peer))
 
     b_step(3)
     b_cross(2)
@@ -304,15 +319,15 @@
     b_relay(1)
     b_relay(-1)
 
-    arrive(rows1)
     i0 = iota((slots, slots), 0)
     order1 = ((i0 >> 2) & (NP - 1)) * 32 + (i0 >> 5) * CAP + (i0 & (CAP - 1))
-    regrouped = dot(bits(order1 == iota((slots, slots), 1)), ra[...].reshape(slots, -1))
-    bb[...] = regrouped.astype(BF).reshape(bb.shape)
-    fb[z] = bb[z]
+    regroup = bits(order1 == iota((slots, slots), 1))
+    for h in halves:
+        arrive(rows1[h])
+        bb[h] = dot(regroup, ra[h].reshape(slots, half_feat)).astype(BF).reshape(bb.shape[1:])
+        rows2.append(spread_out(bb.at[h], fb.at[h], z, NZ, z_peer))
     tool_sends = [send(tools, toolsb.at[c * NYH + yh], y_peer(o)) for o in range(1, NYH)]
     tool_swaps = [send(tools, toolsb.at[c * NYH + yh], other_core)]
-    rows2 = [send(bb.at[lax.rem(z + o, NZ)], fb.at[z], z_peer(o)) for o in range(1, NZ)]
 
     b_step(4)
     b_cross(3)
@@ -334,9 +349,10 @@
     bias_mat[...] = dot(bias_rows.astype(BF), lane_to)
     queries_load.wait()
 
-    arrive(rows2)
+    arrive(rows2[0] + rows2[1])
     select = bits(owner * CAP + rank == iota((chains, slots), 1))
-    combined = queries[...].astype(F32) + dot(select, fb[...].reshape(slots, -1))
+    first_rows = [dot(select, fb[h].reshape(slots, half_feat)) for h in halves]
+    combined = queries[...].astype(F32) + jnp.concatenate(first_rows, axis=1)
     centred = combined - jnp.mean(combined, axis=1, keepdims=True)
     spread_sq = jnp.mean(centred * centred, axis=1, keepdims=True)
     normed = centred * lax.rsqrt(spread_sq + 1e-05) * gain
@@ -371,9 +387,9 @@
     swap_p = send(pbuf.at[1 - c], rbuf, other_core)
     arrive([swap_p])
     updated = (combined + (pbuf[c] + rbuf[...]) + bias_out).astype(BF)
-    updated_ref[...] = updated
     updb[c] = updated
     swap_u = send(updb.at[c], updb.at[c], other_core)
+    updated_out = load(updb.at[c], updated_hbm, 13)
 
     arrive(tool_swaps)
     own_tools.wait()
@@ -397,31 +413,31 @@
     i1 = iota((half, half), 0)
     order2 = ((i1 >> 3) & (NYH - 1)) * 64 + (i1 >> 5) * 8 + (i1 & 7)
     grad_t = dot_t(bits(order2 == iota((half, half), 1)), wga[...].reshape(2 * chains, half)).astype(BF)
-    part = dot(grad_t, updb[...].reshape(2 * chains, -1))
-    s1b[...] = part.astype(BF).reshape(s1b.shape)
-    s1r[p] = s1b[p]
-    stage1 = [send(s1b.at[lax.rem(p + o, NP)], s1r.at[p], p_peer(o)) for o in range(1, NP)]
+    stage1, stage2, stage3, stage4 = [], [], [], []
+    for h in halves:
+        part = dot(grad_t, updb[:, :, cuts[h]].reshape(2 * chains, half_feat))
+        s1b[h] = part.astype(BF).reshape(s1b.shape[1:])
+        stage1.append(spread_out(s1b.at[h], s1r.at[h], p, NP, p_peer))
     loss_ref[...] = jnp.sum(jnp.where(eye, loss, 0.0), axis=0, keepdims=True)
-    qgrad_ref[...] = dot(grad, all_tools)
-    arrive(stage1)
-    total = s1r[0].astype(F32)
-    for i in range(1, NP):
-        total = total + s1r[i].astype(F32)
-    s2b[...] = total.reshape(s2b.shape).astype(BF)
-    s2r[yh] = s2b[yh]
-    arrive([send(s2b.at[lax.rem(yh + o, NYH)], s2r.at[yh], y_peer(o)) for o in range(1, NYH)])
-    total = s2r[0].astype(F32)
-    for i in range(1, NYH):
-        total = total + s2r[i].astype(F32)
-    s3b[...] = total.astype(BF)
-    s3r[z] = s3b[...]
-    arrive([send(s3b, s3r.at[z], z_peer(o)) for o in range(1, NZ)])
-    total = s3r[0].astype(F32)
-    for i in range(1, NZ):
-        total = total + s3r[i].astype(F32)
-    s4r[p] = (total * grad_scale).astype(BF)
-    arrive([send(s4r.at[p], s4r.at[p], p_peer(o)) for o in range(1, NP)])
-    tgrad_ref[...] = s4r[...].astype(F32).reshape(tgrad_ref.shape)
+    qgrad_buf[...] = dot(grad, all_tools)
+    qgrad_out = load(qgrad_buf, qgrad_hbm, 14)
+    for h in halves:
+        arrive(stage1[h])
+        s2b[h] = added(s1r.at[h], NP).astype(BF).reshape(s2b.shape[1:])
+        stage2.append(spread_out(s2b.at[h], s2r.at[h], yh, NYH, y_peer))
+    for h in halves:
+        arrive(stage2[h])
+        s3r[h, z] = added(s2r.at[h], NYH).astype(BF)
+        stage3.append([send(s3r.at[h, z], s3r.at[h, z], z_peer(o)) for o in range(1, NZ)])
+    for h in halves:
+        arrive(stage3[h])
+        s4r[h, p] = (added(s3r.at[h], NZ) * grad_scale).astype(BF)
+        stage4.append([send(s4r.at[h, p], s4r.at[h, p], p_peer(o)) for o in range(1, NP)])
+    for h in halves:
+        arrive(stage4[h])
+        tgrad_ref[:, cuts[h]] = s4r[h].astype(F32).reshape(-1, half_feat)
+    updated_out.wait()
+    qgrad_out.wait()
 
     for copy in started:
         copy.wait_send()
@@ -452,6 +468,7 @@
         block = tools.shape[0]
         scale = (block * mesh.shape["dp"] / (n * mesh.shape["dp"] * mesh.shape["mp"])) ** 0.5
         vmem = pl.BlockSpec(memory_space=pltpu.VMEM)
+        hbm = pl.BlockSpec(memory_space=pltpu.HBM)
         slot_rows = NP * CAP
         sub = block // NP
         scratch = [
@@ -470,26 +487,26 @@
             pltpu.VMEM((NZ, 16, 128), F32),
             pltpu.VMEM((16, 128), F32),
             pltpu.VMEM((NP, 16, 128), F32),
-            pltpu.VMEM((NP, slot_rows, feat), BF),
-            pltpu.VMEM((NP, slot_rows, feat), BF),
-            pltpu.VMEM((NZ, slot_rows, feat), BF),
-            pltpu.VMEM((NZ, slot_rows, feat), BF),
+            pltpu.VMEM((2, NP, slot_rows, feat // 2), BF),
+            pltpu.VMEM((2, NP, slot_rows, feat // 2), BF),
+            pltpu.VMEM((2, NZ, slot_rows, feat // 2), BF),
+            pltpu.VMEM((2, NZ, slot_rows, feat // 2), BF),
             pltpu.VMEM((NC, n, feat), BF),
             pltpu.VMEM((NC, n, feat), F32),
             pltpu.VMEM((n, feat), F32),
             pltpu.VMEM((NC, n, feat), BF),
             pltpu.VMEM((NC, n, NYH * block), BF),
             pltpu.VMEM((NC, n, NYH * block), BF),
-            pltpu.VMEM((NP, NYH * sub, feat), BF),
-            pltpu.VMEM((NP, NYH * sub, feat), BF),
-            pltpu.VMEM((NYH, sub, feat), BF),
-            pltpu.VMEM((NYH, sub, feat), BF),
-            pltpu.VMEM((sub, feat), BF),
-            pltpu.VMEM((NZ, sub, feat), BF),
-            pltpu.VMEM((NP, sub, feat), BF),
+            pltpu.VMEM((2, NP, NYH * sub, feat // 2), BF),
+            pltpu.VMEM((2, NP, NYH * sub, feat // 2), BF),
+            pltpu.VMEM((2, NYH, sub, feat // 2), BF),
+            pltpu.VMEM((2, NYH, sub, feat // 2), BF),
+            pltpu.VMEM((2, NZ, sub, feat // 2), BF),
+            pltpu.VMEM((2, NP, sub, feat // 2), BF),
+            pltpu.VMEM((n, feat), F32),
             pltpu.SemaphoreType.DMA((N_SEMS,)),
             pltpu.SemaphoreType.DMA((N_SEMS,)),
-            pltpu.SemaphoreType.DMA((13,)),
+            pltpu.SemaphoreType.DMA((15,)),
         ]
         updated, loss, qgrad, tgrad = pl.pallas_call(
             functools.partial(kernel, scale),
@@ -500,7 +517,7 @@
                 jax.ShapeDtypeStruct((block, feat), F32),
             ),
             in_specs=[pl.BlockSpec(memory_space=pltpu.HBM)] * 11,
-            out_specs=(vmem,) * 4,
+            out_specs=(hbm, vmem, hbm, vmem),
             scratch_shapes=scratch,
             compiler_params=pltpu.CompilerParams(
                 collective_id=0, has_side_effects=True, vmem_limit_bytes=63 << 20
@@ -519,7 +536,6 @@
             bias_in,
         )
         results = (updated, loss, qgrad, tgrad)
-        hbm = pl.BlockSpec(memory_space=pltpu.HBM)
         updated, loss, qgrad, tgrad = pl.pallas_call(
             hand_over,
             out_shape=tuple(jax.ShapeDtypeStruct(r.shape, r.dtype) for r in results),

time: 88.7 us -> 86.5 us (0.975)
  Pallas kernels: 87.8 us -> 85.7 us
    pallas_call x1, Pallas kernels: 85.8 us -> 83.7 us  [local(): pl.pallas_call(functools.partial(kernel, scale), out_shape=(jax.ShapeDtyp...]
where the time goes in v4:
time: 86.5 us; the launch traced here: 86.3 us
  Pallas kernels  85.7 us (99%)
    pallas_call x1, Pallas kernels, local(): pl.pallas_call(functools.partial(kernel, scale), out_shape=(jax.ShapeDtyp...  83.7 us
    pallas_call x1, Pallas kernels, local(): pl.pallas_call(hand_over, out_shape=tuple((jax.ShapeDtypeStruct(r.shape,...  1.98 us

profile of v4, /device:TPU:2, one launch (start us, length us, event | category | flops | bytes accessed | tf_op | source)
XLA Modules:
  0.0 86.3 jit_solution(9872749266728529682)
XLA Ops:
  0.6 83.7 %shard_map.138 = (bf16[128,768]{1,0:T(8,128)(2,1)}, f32[1,128]{1,0:T(1,128)}, f32[128,768]{1,0:T(8,128)}, f32[64,768]{1,0:T(8,128)}) custom-call(bf16[128,768]{1,0:T(8,128)(2,1)} %queries_hbm.1, s32[1,128]{1,0:T(1,128)} %bitcast.4, s32[1,128]{1,0:T(1,128)} %bitcast.5, s32[1,128]{1,0:T(1,128)} %bitcast.6, bf16[256,768]{1,0:T(8,128)(2,1)} %table_hbm.1, ...), custom_call_target="tpu_custom_call" | custom-call | tf_op jit(solution)/shard_map/pallas_call | solution.py:511
  84.3 2.0 %shard_map.139 = (bf16[128,768]{1,0:T(8,128)(2,1)}, f32[1,128]{1,0:T(1,128)}, f32[128,768]{1,0:T(8,128)}, f32[64,768]{1,0:T(8,128)}) custom-call(bf16[128,768]{1,0:T(8,128)(2,1)} %get-tuple-element.12.refs_0_, f32[1,128]{1,0:T(1,128)} %get-tuple-element.13.refs_1_, f32[128,768]{1,0:T(8,128)} %get-tuple-element.14.refs_2_, f32[64,768]{1,0:T(8,128)} %get-tuple-element.15.refs_3_), custom_call_target="tpu_custom_call" | custom-call | tf_op jit(solution)/shard_map/pallas_call | solution.py:539

commit v5 on v4

--- a/solution.py
+++ b/solution.py
@@ -316,6 +316,8 @@
     b_cross(-2)
     a_step(2, 0)
     a_step(2, 1)
+    a_step(2, 2)
+    a_step(2, 3)
     b_relay(1)
     b_relay(-1)
 
@@ -332,8 +334,6 @@
     b_step(4)
     b_cross(3)
     b_cross(-3)
-    a_step(2, 2)
-    a_step(2, 3)
     b_relay(2)
     b_relay(-2)
     b_cross(4)

time: 86.5 us -> 85.7 us (level)
  no operation moved by 1% of the time
where the time goes in v5:
time: 85.7 us; the launch traced here: 85.5 us
  Pallas kernels  84.9 us (99%)
    pallas_call x1, Pallas kernels, local(): pl.pallas_call(functools.partial(kernel, scale), out_shape=(jax.ShapeDtyp...  82.9 us
    pallas_call x1, Pallas kernels, local(): pl.pallas_call(hand_over, out_shape=tuple((jax.ShapeDtypeStruct(r.shape,...  1.98 us

profile of v5, /device:TPU:2, one launch (start us, length us, event | category | flops | bytes accessed | tf_op | source)
XLA Modules:
  0.0 85.5 jit_solution(578923273663573300)
XLA Ops:
  0.6 82.9 %shard_map.138 = (bf16[128,768]{1,0:T(8,128)(2,1)}, f32[1,128]{1,0:T(1,128)}, f32[128,768]{1,0:T(8,128)}, f32[64,768]{1,0:T(8,128)}) custom-call(bf16[128,768]{1,0:T(8,128)(2,1)} %queries_hbm.1, s32[1,128]{1,0:T(1,128)} %bitcast.4, s32[1,128]{1,0:T(1,128)} %bitcast.5, s32[1,128]{1,0:T(1,128)} %bitcast.6, bf16[256,768]{1,0:T(8,128)(2,1)} %table_hbm.1, ...), custom_call_target="tpu_custom_call" | custom-call | tf_op jit(solution)/shard_map/pallas_call | solution.py:511
  83.5 2.0 %shard_map.139 = (bf16[128,768]{1,0:T(8,128)(2,1)}, f32[1,128]{1,0:T(1,128)}, f32[128,768]{1,0:T(8,128)}, f32[64,768]{1,0:T(8,128)}) custom-call(bf16[128,768]{1,0:T(8,128)(2,1)} %get-tuple-element.12.refs_0_, f32[1,128]{1,0:T(1,128)} %get-tuple-element.13.refs_1_, f32[128,768]{1,0:T(8,128)} %get-tuple-element.14.refs_2_, f32[64,768]{1,0:T(8,128)} %get-tuple-element.15.refs_3_), custom_call_target="tpu_custom_call" | custom-call | tf_op jit(solution)/shard_map/pallas_call | solution.py:539

commit v6 on v5

--- a/solution.py
+++ b/solution.py
@@ -290,6 +290,8 @@
         req2[NZ + zz : NZ + zz + 1, :] = tile[NZ : NZ + 1, :]
     rcv2[p] = req2[...]
     reqs2 = [send(req2, rcv2.at[p], p_peer(o)) for o in range(1, NP)]
+    tool_sends = [send(tools, toolsb.at[c * NYH + yh], y_peer(o)) for o in range(1, NYH)]
+    tool_swaps = [send(tools, toolsb.at[c * NYH + yh], other_core)]
 
     b_step(2)
     b_cross(1)
@@ -328,8 +330,6 @@
         arrive(rows1[h])
         bb[h] = dot(regroup, ra[h].reshape(slots, half_feat)).astype(BF).reshape(bb.shape[1:])
         rows2.append(spread_out(bb.at[h], fb.at[h], z, NZ, z_peer))
-    tool_sends = [send(tools, toolsb.at[c * NYH + yh], y_peer(o)) for o in range(1, NYH)]
-    tool_swaps = [send(tools, toolsb.at[c * NYH + yh], other_core)]
 
     b_step(4)
     b_cross(3)

time: 85.7 us -> 85 us (level)
  no operation moved by 1% of the time
where the time goes in v6:
time: 85 us; the launch traced here: 84.8 us
  Pallas kernels  84.2 us (99%)
    pallas_call x1, Pallas kernels, local(): pl.pallas_call(functools.partial(kernel, scale), out_shape=(jax.ShapeDtyp...  82.2 us
    pallas_call x1, Pallas kernels, local(): pl.pallas_call(hand_over, out_shape=tuple((jax.ShapeDtypeStruct(r.shape,...  1.98 us

profile of v6, /device:TPU:2, one launch (start us, length us, event | category | flops | bytes accessed | tf_op | source)
XLA Modules:
  0.0 84.8 jit_solution(12245238192038475005)
XLA Ops:
  0.6 82.2 %shard_map.138 = (bf16[128,768]{1,0:T(8,128)(2,1)}, f32[1,128]{1,0:T(1,128)}, f32[128,768]{1,0:T(8,128)}, f32[64,768]{1,0:T(8,128)}) custom-call(bf16[128,768]{1,0:T(8,128)(2,1)} %queries_hbm.1, s32[1,128]{1,0:T(1,128)} %bitcast.4, s32[1,128]{1,0:T(1,128)} %bitcast.5, s32[1,128]{1,0:T(1,128)} %bitcast.6, bf16[256,768]{1,0:T(8,128)(2,1)} %table_hbm.1, ...), custom_call_target="tpu_custom_call" | custom-call | tf_op jit(solution)/shard_map/pallas_call | solution.py:511
  82.8 2.0 %shard_map.139 = (bf16[128,768]{1,0:T(8,128)(2,1)}, f32[1,128]{1,0:T(1,128)}, f32[128,768]{1,0:T(8,128)}, f32[64,768]{1,0:T(8,128)}) custom-call(bf16[128,768]{1,0:T(8,128)(2,1)} %get-tuple-element.12.refs_0_, f32[1,128]{1,0:T(1,128)} %get-tuple-element.13.refs_1_, f32[128,768]{1,0:T(8,128)} %get-tuple-element.14.refs_2_, f32[64,768]{1,0:T(8,128)} %get-tuple-element.15.refs_3_), custom_call_target="tpu_custom_call" | custom-call | tf_op jit(solution)/shard_map/pallas_call | solution.py:539
